TPU v7x, 32 devices: a whole 2x2x4 slice. The times are simulated.
32 devices in a mesh: param: 4 (over x, core), space: 8 (over z, y).
Axes of the slice: x: 2, y: 2, z: 4, core: 2. Of those that a mesh axis runs over, the one named last changes fastest.
Arguments:
- fine_state: bfloat16 [16, 16, 64, 512], P('space', None, None, 'param'), may hold values from -6 to 6
- fine_tangent: bfloat16 [16, 16, 64, 512], P('space', None, None, 'param'), may hold values from -6 to 6
- down_weight: float32 [8, 512, 1024], P(None, 'space', 'param'), may hold values from -0.09375 to 0.09375
- conv_weight: float32 [27, 1024, 1024], P(None, 'space', 'param'), may hold values from -0.0390625 to 0.0390625
- up_weight: float32 [8, 1024, 512], P(None, 'space', 'param'), may hold values from -0.1875 to 0.1875
Outputs:
- state_out: bfloat16 [16, 16, 64, 512], P('space', None, None, 'param')
- tangent_out: bfloat16 [16, 16, 64, 512], P('space', None, None, 'param')
All inputs are finite; a program needn't handle non-finite values.
Results may differ from a plain program's by a relative error of at most 0.0075.
Values may be sent and summed in bfloat16 or wider, within the bound.
No kernel may reach another device: no remote copies, remote signals or barrier semaphores. Data moves between devices by JAX's collectives and lax.ppermute only.
A program may use at most 128 MiB of HBM per device.

v0:
```python
import jax
import jax.numpy as jnp
from jax import lax
from jax.sharding import PartitionSpec as P


def padded(block, sides, width):
    for axis, dim in sides:
        count = lax.axis_size(axis)
        forward = [(i, i + 1) for i in range(count - 1)]
        backward = [(target, source) for source, target in forward]
        low = lax.ppermute(
            lax.slice_in_dim(block, block.shape[dim] - width, None, axis=dim), axis, forward
        )
        high = lax.ppermute(lax.slice_in_dim(block, 0, width, axis=dim), axis, backward)
        block = jnp.concatenate([low, block, high], axis=dim)
    return block


def partner(block, axis, apart):
    count = lax.axis_size(axis)
    route = []
    for low in range(count):
        high = low | 1 << apart
        if high != low and high < count:
            route += [(low, high), (high, low)]
    return lax.ppermute(block, axis, route)


def silu_pair(primal, tangent):
    sigma = jax.nn.sigmoid(primal)
    return (primal * sigma, sigma * (1.0 + primal * (1.0 - sigma)) * tangent)


def cube_block(source, kernel, planes):
    span_y = source.shape[2] - 2
    span_x = source.shape[3] - 2
    width = source.shape[4]
    result = None
    for tap_z in range(3):
        for tap_y in range(3):
            window = jnp.stack(
                [
                    source[
                        :, tap_z : tap_z + planes, tap_y : tap_y + span_y, tap_x : tap_x + span_x, :
                    ]
                    for tap_x in range(3)
                ],
                axis=4,
            )
            window = window.reshape(-1, 3 * width)
            first_tap = 9 * tap_z + 3 * tap_y
            weights = kernel[first_tap : first_tap + 3].reshape(3 * width, kernel.shape[2])
            term = jnp.dot(window, weights, preferred_element_type=jnp.float32)
            result = term if result is None else result + term
    return result


def local(fine_state, fine_tangent, down_weight, conv_weight, up_weight):
    planes = fine_state.shape[0] // 2
    span_y = fine_state.shape[1] // 2
    span_x = fine_state.shape[2] // 2
    cells = planes * span_y * span_x
    state_full, tangent_full = (
        lax.all_gather(fine_state, "param", axis=3, tiled=True),
        lax.all_gather(fine_tangent, "param", axis=3, tiled=True),
    )
    wide_fine = state_full.shape[3]
    paired = jnp.stack([state_full, tangent_full], axis=0)
    patches = (
        paired.reshape(2, planes, 2, span_y, 2, span_x, 2, wide_fine)
        .transpose(0, 1, 3, 5, 2, 4, 6, 7)
        .reshape(2 * cells, 8, wide_fine)
    )
    down_kernel = down_weight.astype(jnp.bfloat16)
    up_kernel = up_weight.astype(jnp.bfloat16)
    cube_kernel = conv_weight.astype(jnp.bfloat16)
    coarse_local = down_weight.shape[2]
    fine_local = up_weight.shape[2]
    portion = lax.all_gather(down_kernel, "space", axis=1, tiled=True)
    width = portion.shape[1]
    columns = patches.reshape(2 * cells, 8 * width)
    first_pre = jnp.dot(
        columns, portion.reshape(8 * width, portion.shape[2]), preferred_element_type=jnp.float32
    )
    first_pre = first_pre.reshape(2, cells, coarse_local)
    first_val, first_dir = silu_pair(first_pre[0], first_pre[1])
    first_round = jnp.stack(
        [first_val.astype(jnp.bfloat16), first_dir.astype(jnp.bfloat16)], axis=0
    )
    first_stack = first_round.reshape(2, planes, span_y, span_x, coarse_local)
    haloed = padded(first_stack, (("space", 1),), 1)
    every_channel = lax.all_gather(haloed, "param", axis=4, tiled=True)
    position = lax.axis_index("space")
    levels = lax.axis_size("space").bit_length() - 1
    wide_coarse = every_channel.shape[4]
    block_kernel = cube_kernel
    for bit in range(levels - 1):
        partner_block = partner(block_kernel, "space", bit)
        upper = position >> bit & 1
        block_kernel = jnp.where(
            upper == 1,
            jnp.concatenate([partner_block, block_kernel], axis=1),
            jnp.concatenate([block_kernel, partner_block], axis=1),
        )
    half_index = position >> levels - 1
    own_half = lax.dynamic_slice_in_dim(
        every_channel, half_index * (wide_coarse // 2), wide_coarse // 2, 4
    )
    send_half = lax.dynamic_slice_in_dim(
        every_channel, (1 - half_index) * (wide_coarse // 2), wide_coarse // 2, 4
    )
    other_half = partner(send_half, "space", levels - 1)
    own_padded = jnp.pad(own_half, ((0, 0), (0, 0), (1, 1), (1, 1), (0, 0)))
    other_padded = jnp.pad(other_half, ((0, 0), (0, 0), (1, 1), (1, 1), (0, 0)))
    own_sum = cube_block(own_padded, block_kernel, planes)
    other_sum = cube_block(other_padded, block_kernel, planes)
    returned = partner(other_sum.astype(jnp.bfloat16), "space", levels - 1).astype(other_sum.dtype)
    second_pre = (own_sum + returned).reshape(2, cells, coarse_local)
    second_val, second_dir = silu_pair(second_pre[0], second_pre[1])
    second_val = second_val + first_round[0].astype(jnp.float32)
    second_dir = second_dir + first_round[1].astype(jnp.float32)
    top_stack = jnp.stack(
        [second_val.astype(jnp.bfloat16), second_dir.astype(jnp.bfloat16)], axis=0
    )
    top_full = lax.all_gather(top_stack, "param", axis=2, tiled=True)
    top_rows = top_full.reshape(2 * cells, top_full.shape[2])
    portion = lax.all_gather(up_kernel, "space", axis=1, tiled=True)
    width = portion.shape[1]
    columns = top_rows
    product = jnp.dot(
        columns,
        portion.transpose(1, 0, 2).reshape(width, 8 * fine_local),
        preferred_element_type=jnp.float32,
    )
    shaped = product.reshape(2, planes, span_y, span_x, 2, 2, 2, fine_local).transpose(
        0, 1, 4, 2, 5, 3, 6, 7
    )
    outputs = shaped.reshape(2, 2 * planes, 2 * span_y, 2 * span_x, fine_local).astype(jnp.bfloat16)
    return (outputs[0], outputs[1])


def solution(mesh):
    in_specs = (
        P("space", None, None, "param"),
        P("space", None, None, "param"),
        P(None, "space", "param"),
        P(None, "space", "param"),
        P(None, "space", "param"),
    )
    out_specs = (P("space", None, None, "param"), P("space", None, None, "param"))
    return jax.shard_map(local, mesh=mesh, in_specs=in_specs, out_specs=out_specs, check_vma=False)
```

profile of v0, /device:TPU:0, one launch (start us, length us, event | category | flops | bytes accessed | tf_op | source)
XLA Modules:
  0.0 400.6 jit_solution(16361517730919954494)
XLA Ops:
  7.2 0.7 all-gather.9.cloned.1.call-update
  7.9 0.7 all-gather.7.cloned.1.call-update
  8.7 1.8 convert_element_type.46
  10.5 3.5 convert_element_type.49
  14.0 3.0 collective-permute-start.2
  17.0 18.1 %all-gather.9.cloned.1.call-done = bf16[2,16,64,512]{3,2,1,0:T(8,128)(2,1)} async-done(((bf16[2,16,64,128]{3,2,1,0:T(8,128)(2,1)}), bf16[2,16,64,512]{3,2,1,0:T(8,128)(2,1)}) %all-gather.9.cloned.1.call-update) | async-done | bytes 2097168 | tf_op jit(solution)/shard_map/all_gather | solution.py:66
  35.1 2.7 stack.244
  37.8 21.6 %all-gather.7.cloned.1.call-done = bf16[2,16,64,512]{3,2,1,0:T(8,128)(2,1)} async-done(((bf16[2,16,64,128]{3,2,1,0:T(8,128)(2,1)}), bf16[2,16,64,512]{3,2,1,0:T(8,128)(2,1)}) %all-gather.7.cloned.1.call-update) | async-done | bytes 2097168 | tf_op jit(solution)/shard_map/all_gather | solution.py:65
  59.5 4.1 %stack.243 = bf16[1,1,2,8,2,32,2,512]{7,6,5,4,3,2,1,0:T(2,128)(2,1)} reshape(bf16[2,16,64,512]{3,2,1,0:T(8,128)(2,1)} %all-gather.7.cloned.1.call-done) | data formatting | bytes 4194304 | tf_op jit(solution)/shard_map/stack | solution.py:69
  63.6 7.8 %copy_bitcast_fusion = bf16[2,1,8,32,2,2,2,512]{7,6,5,4,3,2,0,1:T(2,128)(2,1)} fusion(bf16[1,1,2,8,2,32,2,512]{7,6,5,4,3,2,1,0:T(2,128)(2,1)S(1)} %stack.244, bf16[1,1,2,8,2,32,2,512]{7,6,5,4,3,2,1,0:T(2,128)(2,1)} %stack.243), kind=kLoop, calls=%fused_computation.50 | loop fusion | flops 2097152 | bytes 8388608 | tf_op jit(solution)/shard_map/transpose | solution.py:72
  71.4 7.8 %reshape_reshape.3 = bf16[512,4096]{1,0:T(8,128)(2,1)} reshape(bf16[2,1,8,32,2,2,2,512]{7,6,5,4,3,2,0,1:T(2,128)(2,1)} %copy_bitcast_fusion) | data formatting | bytes 8388608 | tf_op jit(solution)/shard_map/reshape;reshape | solution.py:82
  79.2 32.2 %all-gather.11.cloned.1.call-done = bf16[8,512,256]{2,1,0:T(8,128)(2,1)} async-done(((bf16[8,64,256]{2,1,0:T(8,128)(2,1)}), bf16[8,512,256]{2,1,0:T(8,128)(2,1)}) %all-gather.11.cloned.1.call-update) | async-done | bytes 2097168 | tf_op jit(solution)/shard_map/all_gather | solution.py:80
  111.4 4.1 %fusion.72 = f32[512,256]{1,0:T(8,128)S(1)} fusion(bf16[512,4096]{1,0:T(8,128)(2,1)} %reshape_reshape.3, bf16[4096,256]{1,0:T(8,128)(2,1)} %bitcast.331), kind=kOutput, calls=%fused_computation.162 | convolution fusion | flops 1073741824 | bytes 6815744 | tf_op jit(solution)/shard_map/dot_general | solution.py:83
  115.7 1.3 collective-permute-start.1
  117.0 4.6 %collective-permute-start = (bf16[2,1,8,32,256]{4,3,2,0,1:T(8,128)(2,1)S(1)}, bf16[2,1,8,32,256]{4,3,2,0,1:T(8,128)(2,1)S(1)}, u32[]{:S(2)}, u32[]{:S(2)}) collective-permute-start(bf16[2,1,8,32,256]{4,3,2,0,1:T(8,128)(2,1)S(1)} %pad_maximum_fusion.20), channel_id=1, source_target_pairs={{0,1},{1,2},{2,3},{3,4},{4,5},{5,6},{6,7},{8,9},{9,10},{10,11},{11... | collective-permute-start | bytes 786440 | tf_op jit(solution)/shard_map/ppermute | solution.py:12
  121.5 2.4 collective-permute-done.1
  123.9 5.0 %collective-permute-done = bf16[2,1,8,32,256]{4,3,2,0,1:T(8,128)(2,1)S(1)} collective-permute-done((bf16[2,1,8,32,256]{4,3,2,0,1:T(8,128)(2,1)S(1)}, bf16[2,1,8,32,256]{4,3,2,0,1:T(8,128)(2,1)S(1)}, u32[]{:S(2)}, u32[]{:S(2)}) %collective-permute-start) | collective-permute-done | bytes 262176 | tf_op jit(solution)/shard_map/ppermute | solution.py:12
  128.9 1.0 pad_maximum_fusion.19
  130.0 4.0 maximum_select_fusion.1
  134.0 2.8 collective-permute-start.3
  136.8 1.9 copy.61
  138.8 99.1 %collective-permute-done.3 = bf16[27,256,256]{2,1,0:T(8,128)(2,1)} collective-permute-done((bf16[27,256,256]{2,1,0:T(8,128)(2,1)S(1)}, bf16[27,256,256]{2,1,0:T(8,128)(2,1)}, u32[]{:S(2)}, u32[]{:S(2)}) %collective-permute-start.3) | collective-permute-done | bytes 3538976 | tf_op jit(solution)/shard_map/ppermute | solution.py:27
  237.9 5.1 %maximum_select_fusion = bf16[27,512,256]{2,1,0:T(8,128)(2,1)S(1)} fusion(bf16[27,256,256]{2,1,0:T(8,128)(2,1)S(1)} %maximum_select_fusion.1, bf16[27,256,256]{2,1,0:T(8,128)(2,1)} %collective-permute-done.3, pred[]{:T(512)S(6)} %eq.6), kind=kLoop, calls=%fused_computation | loop fusion | flops 31850496 | bytes 14155777 | tf_op jit(solution)/shard_map/jit(_where)/select_n | solution.py:101
  243.0 1.9 fusion.70
  245.0 2.3 constant_dynamic-slice_fusion
  247.7 4.1 %fusion.17 = (bf16[2,1,8,32,1,512]{5,3,2,0,4,1:T(8,128)(2,1)S(1)}, bf16[2,1,8,32,1,512]{5,3,2,0,4,1:T(8,128)(2,1)S(1)}, bf16[2,1,8,32,1,512]{5,3,2,0,4,1:T(8,128...) fusion(bf16[2,3,8,32,512]{4,3,2,0,1:T(8,128)(2,1)S(1)} %get-tup, ...), kind=kLoop, calls=%fused_computation.91 | loop fusion | bytes 11534336 | tf_op jit(solution)/shard_map/stack | solution.py:42
  252.4 1.4 copy.51
  254.3 1.4 copy.50
  256.2 2.5 collective-permute-start.4
  259.3 0.6 fusion.79
  261.1 1.4 copy.49
  263.0 1.4 copy.48
  264.9 1.8 copy.47
  267.2 1.4 copy.46
  269.1 1.4 copy.45
  271.0 1.4 copy.44
  272.9 1.4 copy.43
  274.9 0.6 copy-done.2
  278.9 46.7 %collective-permute-done.4 = bf16[2,3,8,32,512]{4,3,2,0,1:T(8,128)(2,1)S(1)} collective-permute-done((bf16[2,3,8,32,512]{4,3,2,0,1:T(8,128)(2,1)S(1)}, bf16[2,3,8,32,512]{4,3,2,0,1:T(8,128)(2,1)S(1)}, u32[]{:S(2)}, u32[]{:S(2)}) %collective-permute-start.4) | collective-permute-done | bytes 1572896 | tf_op jit(solution)/shard_map/ppermute | solution.py:27
  326.5 1.5 copy.60
  329.2 1.4 copy.59
  331.1 3.9 fusion.41
  335.2 1.4 copy.58
  337.5 1.4 copy.57
  339.7 1.4 copy.56
  341.6 1.4 copy.55
  343.9 1.4 copy.54
  345.8 1.6 copy.53
  347.9 1.4 copy.52
  349.8 0.6 fusion.87
  350.4 0.6 fusion.86
  350.9 0.6 fusion.85
  351.5 0.6 fusion.84
  352.1 0.6 fusion.83
  352.7 0.6 fusion.82
  353.3 0.6 fusion.81
  353.8 0.7 fusion.16
  355.2 11.3 %collective-permute-done.5 = bf16[512,256]{1,0:T(8,128)(2,1)S(1)} collective-permute-done((bf16[512,256]{1,0:T(8,128)(2,1)S(1)}, bf16[512,256]{1,0:T(8,128)(2,1)S(1)}, u32[]{:S(2)}, u32[]{:S(2)}) %collective-permute-start.5) | collective-permute-done | bytes 262176 | tf_op jit(solution)/shard_map/ppermute | solution.py:27
  366.5 0.7 fusion.15
  367.7 0.7 pad_maximum_fusion.21
  368.4 19.1 %all-gather.15.cloned.1.call-done = bf16[2,256,1024]{2,1,0:T(8,128)(2,1)} async-done(((bf16[2,256,256]{2,1,0:T(8,128)(2,1)}), bf16[2,256,1024]{2,1,0:T(8,128)(2,1)}) %all-gather.15.cloned.1.call-update) | async-done | bytes 1048592 | tf_op jit(solution)/shard_map/all_gather | solution.py:126
  387.6 3.2 fusion
  390.9 1.3 copy.62
  392.2 1.3 copy.63
  (76 shorter events, 20.1 us)
Async XLA Ops:
  7.2 27.9 %all-gather.9.cloned.1.call-start = ((), (), s32[]{:S(2)}) async-start(), calls=%async_computation.1 | async-start | bytes 2621440 | tf_op jit(solution)/shard_map/all_gather | solution.py:66
  7.9 51.6 %all-gather.7.cloned.1.call-start = ((), (), s32[]{:S(2)}) async-start(), calls=%async_computation | async-start | bytes 2621440 | tf_op jit(solution)/shard_map/all_gather | solution.py:65
  8.6 102.7 %all-gather.11.cloned.1.call-start = ((), (), s32[]{:S(2)}) async-start(), calls=%async_computation.2 | async-start | bytes 2359296 | tf_op jit(solution)/shard_map/all_gather | solution.py:80
  10.5 234.5 %all-gather.13.cloned.1.call-start = ((), (), s32[]{:S(2)}) async-start(), calls=%async_computation.3 | async-start | bytes 3932160 | tf_op jit(solution)/shard_map/all_gather | solution.py:93
  14.0 115.9 %collective-permute-start.2 = (bf16[27,128,256]{2,1,0:T(8,128)(2,1)}, bf16[27,128,256]{2,1,0:T(8,128)(2,1)}, u32[]{:S(2)}, u32[]{:S(2)}) collective-permute-start(bf16[27,128,256]{2,1,0:T(8,128)(2,1)} %convert_element_type.49), channel_id=1, source_target_pairs={{0,1},{1,0},{2,3},{3,2},{4,5},{5,4},{6,7},{7,6},{8,9},{9,8},{10,11... | collective-permute-start | bytes 5308424 | tf_op jit(solution)/shard_map/ppermute | solution.py:27
  115.6 13.3 %copy-start.6 = (bf16[256,256]{1,0:T(8,128)(2,1)}, bf16[256,256]{1,0:T(8,128)(2,1)S(1)}, u32[]{:S(2)}) copy-start(bf16[256,256]{1,0:T(8,128)(2,1)S(1)} %get-tuple-element.71) | copy-start | bytes 393220
  115.6 13.3 %copy-start.8 = (bf16[256,256]{1,0:T(8,128)(2,1)}, bf16[256,256]{1,0:T(8,128)(2,1)S(1)}, u32[]{:S(2)}) copy-start(bf16[256,256]{1,0:T(8,128)(2,1)S(1)} %get-tuple-element.72) | copy-start | bytes 393220
  115.7 8.3 %collective-permute-start.1 = (bf16[2,1,8,32,256]{4,3,2,0,1:T(8,128)(2,1)S(1)}, bf16[2,1,8,32,256]{4,3,2,0,1:T(8,128)(2,1)S(1)}, u32[]{:S(2)}, u32[]{:S(2)}) collective-permute-start(bf16[2,1,8,32,256]{4,3,2,0,1:T(8,128)(2,1)S(1)} %pad_maximum_fusion.20), channel_id=1, source_target_pairs={{1,0},{2,1},{3,2},{4,3},{5,4},{6,5},{7,6},{9,8},{10,9},{11,10},{12... | collective-permute-start | bytes 786440 | tf_op jit(solution)/shard_map/ppermute | solution.py:15
  117.0 12.0 %collective-permute-start = (bf16[2,1,8,32,256]{4,3,2,0,1:T(8,128)(2,1)S(1)}, bf16[2,1,8,32,256]{4,3,2,0,1:T(8,128)(2,1)S(1)}, u32[]{:S(2)}, u32[]{:S(2)}) collective-permute-start(bf16[2,1,8,32,256]{4,3,2,0,1:T(8,128)(2,1)S(1)} %pad_maximum_fusion.20), channel_id=1, source_target_pairs={{0,1},{1,2},{2,3},{3,4},{4,5},{5,6},{6,7},{8,9},{9,10},{10,11},{11... | collective-permute-start | bytes 786440 | tf_op jit(solution)/shard_map/ppermute | solution.py:12
  129.9 238.5 %all-gather.17.cloned.1.call-start = ((), (), s32[]{:S(2)}) async-start(), calls=%async_computation.5 | async-start | bytes 2359296 | tf_op jit(solution)/shard_map/all_gather | solution.py:128
  134.0 103.9 %collective-permute-start.3 = (bf16[27,256,256]{2,1,0:T(8,128)(2,1)S(1)}, bf16[27,256,256]{2,1,0:T(8,128)(2,1)}, u32[]{:S(2)}, u32[]{:S(2)}) collective-permute-start(bf16[27,256,256]{2,1,0:T(8,128)(2,1)S(1)} %maximum_select_fusion.1), channel_id=1, source_target_pairs={{0,2},{2,0},{1,3},{3,1},{4,6},{6,4},{5,7},{7,5},{8,10},{10,8},{9,1... | collective-permute-start | bytes 10616840 | tf_op jit(solution)/shard_map/ppermute | solution.py:27
  138.7 248.8 %all-gather.15.cloned.1.call-start = ((), (), s32[]{:S(2)}) async-start(), calls=%async_computation.4 | async-start | bytes 1310720 | tf_op jit(solution)/shard_map/all_gather | solution.py:126
  247.7 4.1 %copy-start.5 = (bf16[2,3,8,32,1024]{4,3,2,0,1:T(8,128)(2,1)S(1)}, bf16[2,3,8,32,1024]{4,3,2,0,1:T(8,128)(2,1)}, u32[]{:S(2)}) copy-start(bf16[2,3,8,32,1024]{4,3,2,0,1:T(8,128)(2,1)} %all-gather.13.cloned.1.call-done) | copy-start | bytes 9437188
  255.6 3.0 copy-start.4
  256.2 3.1 copy-start.3
  256.2 69.4 %collective-permute-start.4 = (bf16[2,3,8,32,512]{4,3,2,0,1:T(8,128)(2,1)S(1)}, bf16[2,3,8,32,512]{4,3,2,0,1:T(8,128)(2,1)S(1)}, u32[]{:S(2)}, u32[]{:S(2)}) collective-permute-start(bf16[2,3,8,32,512]{4,3,2,0,1:T(8,128)(2,1)S(1)} %get-tuple-element.11), channel_id=1, source_target_pairs={{0,4},{4,0},{1,5},{5,1},{2,6},{6,2},{3,7},{7,3},{8,12},{12,8},{9,1... | collective-permute-start | bytes 4718600 | tf_op jit(solution)/shard_map/ppermute | solution.py:27
  274.3 1.1 copy-start.2
  274.9 1.2 copy-start.1
  276.0 1.1 copy-start
  354.6 11.9 %collective-permute-start.5 = (bf16[512,256]{1,0:T(8,128)(2,1)S(1)}, bf16[512,256]{1,0:T(8,128)(2,1)S(1)}, u32[]{:S(2)}, u32[]{:S(2)}) collective-permute-start(bf16[512,256]{1,0:T(8,128)(2,1)S(1)} %fusion.16), channel_id=1, source_target_pairs={{0,4},{4,0},{1,5},{5,1},{2,6},{6,2},{3,7},{7,3},{8,12},{12,8},{9,1... | collective-permute-start | bytes 786440 | tf_op jit(solution)/shard_map/ppermute | solution.py:27
  366.5 0.9 copy-start.7
  366.5 1.0 copy-start.9
Sparse Core Ops, SparseCore 0:
  9.5 25.5 all-gather.8
  36.6 22.8 all-gather.6
  62.3 49.0 all-gather.10
  130.1 29.8 all-gather.12
  162.4 67.9 all-gather.16
  368.5 19.0 all-gather.14
where the time goes:
time: 407 us; the launch traced here: 401 us
  waiting for transfers between devices  257 us (63%)
  local copies, waits for them, and re-layouts  69.1 us (17%)
  other arithmetic  27.3 us (7%)
  matrix products  17.8 us (4%)
  between operations  15.1 us (4%)
  starting transfers between devices  14.5 us (4%)
    ppermute x4, waiting for transfers between devices, partner(): return lax.ppermute(block, axis, route)  157 us
    another operation x23, local copies, waits for them, and re-layouts, cube_block(): jnp.stack([source[:, tap_z:tap_z + planes, tap_y:tap_y + span_y, tap_x:ta...  34.6 us
    all_gather x1, waiting for transfers between devices, local(): portion = lax.all_gather(down_kernel, 'space', axis=1, tiled=True)  32.2 us
    all_gather x1, waiting for transfers between devices, local(): lax.all_gather(fine_state, 'param', axis=3, tiled=True)  21.6 us
    all_gather x1, waiting for transfers between devices, local(): top_full = lax.all_gather(top_stack, 'param', axis=2, tiled=True)  19.1 us
    all_gather x1, waiting for transfers between devices, local(): lax.all_gather(fine_tangent, 'param', axis=3, tiled=True)  18.1 us
    unnamed x39, local copies, waits for them, and re-layouts  12.9 us
    dot_general x18, matrix products, cube_block(): term = jnp.dot(window, weights, preferred_element_type=jnp.float32)  10.5 us
  transfers between devices with their start and end apart: 12, of which 9 were waited for; matrix products, arithmetic and copies ran while one was open for 27% of the time, Pallas kernels for 0%

commit v1 on v0

--- a/solution.py
+++ b/solution.py
@@ -77,7 +77,14 @@
     cube_kernel = conv_weight.astype(jnp.bfloat16)
     coarse_local = down_weight.shape[2]
     fine_local = up_weight.shape[2]
-    portion = lax.all_gather(down_kernel, "space", axis=1, tiled=True)
+    ring = [down_kernel]
+    for hop in range(7):
+        ring.append(lax.ppermute(ring[-1], "space", [(dev, (dev + 1) % 8) for dev in range(8)]))
+    portion = jnp.roll(
+        jnp.concatenate(ring[::-1], axis=1),
+        (lax.axis_index("space") + 1) * ring[0].shape[1],
+        axis=1,
+    )
     width = portion.shape[1]
     columns = patches.reshape(2 * cells, 8 * width)
     first_pre = jnp.dot(

time: 407 us -> 387 us (0.951)
  waiting for transfers between devices: 257 us -> 238 us
    ppermute x0 -> x7, waiting for transfers between devices: none -> 62.2 us  [local(): lax.ppermute(ring[-1], 'space', [(dev, (dev + 1) % 8) for dev in range(8)])]
    all_gather x1 -> x0, waiting for transfers between devices: 32.2 us -> none  [local(): portion = lax.all_gather(down_kernel, 'space', axis=1, tiled=True)]
    all_gather x1, waiting for transfers between devices: 21.6 us -> 0.02 us  [local(): lax.all_gather(fine_state, 'param', axis=3, tiled=True)]
    all_gather x1, waiting for transfers between devices: 18.1 us -> 0.01 us  [local(): lax.all_gather(fine_tangent, 'param', axis=3, tiled=True)]
    ppermute x4, waiting for transfers between devices: 157 us -> 148 us  [partner(): return lax.ppermute(block, axis, route)]
    ppermute x4, starting transfers between devices: 8.36 us -> 1.48 us  [partner(): return lax.ppermute(block, axis, route)]
    unnamed x39 -> x57, local copies, waits for them, and re-layouts: 12.9 us -> 14.6 us
  transfers between devices with their start and end apart: 12 -> 18, of which waited for: 9 -> 13; matrix products, arithmetic and copies ran while one was open for 27% -> 28% of each run, Pallas kernels for 0% -> 0%
where the time goes in v1:
time: 387 us; the launch traced here: 380 us
  waiting for transfers between devices  238 us (61%)
  local copies, waits for them, and re-layouts  72.4 us (19%)
  other arithmetic  26.8 us (7%)
  matrix products  17.1 us (4%)
  between operations  15 us (4%)
  starting transfers between devices  10.6 us (3%)
    ppermute x4, waiting for transfers between devices, partner(): return lax.ppermute(block, axis, route)  148 us
    ppermute x7, waiting for transfers between devices, local(): lax.ppermute(ring[-1], 'space', [(dev, (dev + 1) % 8) for dev in range(8)])  62.2 us
    another operation x23, local copies, waits for them, and re-layouts, cube_block(): jnp.stack([source[:, tap_z:tap_z + planes, tap_y:tap_y + span_y, tap_x:ta...  34.6 us
    all_gather x1, waiting for transfers between devices, local(): top_full = lax.all_gather(top_stack, 'param', axis=2, tiled=True)  21 us
    unnamed x57, local copies, waits for them, and re-layouts  14.6 us
    dot_general x18, matrix products, cube_block(): term = jnp.dot(window, weights, preferred_element_type=jnp.float32)  10.5 us
    select_n x2, other arithmetic, local(): jnp.where(upper == 1, jnp.concatenate([partner_block, block_kernel], axis...  9.22 us
    another operation x1, local copies, waits for them, and re-layouts, local(): columns = patches.reshape(2 * cells, 8 * width)  8 us
  transfers between devices with their start and end apart: 18, of which 13 were waited for; matrix products, arithmetic and copies ran while one was open for 28% of the time, Pallas kernels for 0%

profile of v1, /device:TPU:0, one launch (start us, length us, event | category | flops | bytes accessed | tf_op | source)
XLA Modules:
  0.0 379.8 jit_solution(18301934233654358013)
XLA Ops:
  7.2 0.7 all-gather.8.cloned.1.call-update
  7.9 1.1 convert_element_type.46
  9.0 3.0 collective-permute-start
  12.1 9.3 %collective-permute-done = bf16[8,64,256]{2,1,0:T(8,128)(2,1)S(1)} collective-permute-done((bf16[8,64,256]{2,1,0:T(8,128)(2,1)S(1)}, bf16[8,64,256]{2,1,0:T(8,128)(2,1)S(1)}, u32[]{:S(2)}, u32[]{:S(2)}) %collective-permute-start) | collective-permute-done | bytes 262176 | tf_op jit(solution)/shard_map/ppermute | solution.py:82
  21.4 10.2 %collective-permute-done.1 = bf16[8,64,256]{2,1,0:T(8,128)(2,1)S(1)} collective-permute-done((bf16[8,64,256]{2,1,0:T(8,128)(2,1)S(1)}, bf16[8,64,256]{2,1,0:T(8,128)(2,1)S(1)}, u32[]{:S(2)}, u32[]{:S(2)}) %collective-permute-start.1) | collective-permute-done | bytes 262176 | tf_op jit(solution)/shard_map/ppermute | solution.py:82
  31.6 9.3 %collective-permute-done.2 = bf16[8,64,256]{2,1,0:T(8,128)(2,1)S(1)} collective-permute-done((bf16[8,64,256]{2,1,0:T(8,128)(2,1)S(1)}, bf16[8,64,256]{2,1,0:T(8,128)(2,1)S(1)}, u32[]{:S(2)}, u32[]{:S(2)}) %collective-permute-start.2) | collective-permute-done | bytes 262176 | tf_op jit(solution)/shard_map/ppermute | solution.py:82
  41.0 9.0 %collective-permute-done.3 = bf16[8,64,256]{2,1,0:T(8,128)(2,1)S(1)} collective-permute-done((bf16[8,64,256]{2,1,0:T(8,128)(2,1)S(1)}, bf16[8,64,256]{2,1,0:T(8,128)(2,1)S(1)}, u32[]{:S(2)}, u32[]{:S(2)}) %collective-permute-start.3) | collective-permute-done | bytes 262176 | tf_op jit(solution)/shard_map/ppermute | solution.py:82
  50.0 9.1 %collective-permute-done.4 = bf16[8,64,256]{2,1,0:T(8,128)(2,1)S(1)} collective-permute-done((bf16[8,64,256]{2,1,0:T(8,128)(2,1)S(1)}, bf16[8,64,256]{2,1,0:T(8,128)(2,1)S(1)}, u32[]{:S(2)}, u32[]{:S(2)}) %collective-permute-start.4) | collective-permute-done | bytes 262176 | tf_op jit(solution)/shard_map/ppermute | solution.py:82
  59.0 9.7 %collective-permute-done.5 = bf16[8,64,256]{2,1,0:T(8,128)(2,1)S(1)} collective-permute-done((bf16[8,64,256]{2,1,0:T(8,128)(2,1)S(1)}, bf16[8,64,256]{2,1,0:T(8,128)(2,1)S(1)}, u32[]{:S(2)}, u32[]{:S(2)}) %collective-permute-start.5) | collective-permute-done | bytes 262176 | tf_op jit(solution)/shard_map/ppermute | solution.py:82
  68.7 3.5 convert_element_type.49
  72.2 5.7 %collective-permute-done.6 = bf16[8,64,256]{2,1,0:T(8,128)(2,1)S(1)} collective-permute-done((bf16[8,64,256]{2,1,0:T(8,128)(2,1)S(1)}, bf16[8,64,256]{2,1,0:T(8,128)(2,1)S(1)}, u32[]{:S(2)}, u32[]{:S(2)}) %collective-permute-start.6) | collective-permute-done | bytes 262176 | tf_op jit(solution)/shard_map/ppermute | solution.py:82
  78.1 0.9 copy-done.6
  79.2 1.5 constant_dynamic-slice_fusion.2
  80.7 2.7 stack.244
  83.5 4.1 %stack.243 = bf16[1,1,2,8,2,32,2,512]{7,6,5,4,3,2,1,0:T(2,128)(2,1)} reshape(bf16[2,16,64,512]{3,2,1,0:T(8,128)(2,1)} %all-gather.6.cloned.1.call-done) | data formatting | bytes 4194304 | tf_op jit(solution)/shard_map/stack | solution.py:69
  87.6 7.8 %copy_bitcast_fusion = bf16[2,1,8,32,2,2,2,512]{7,6,5,4,3,2,0,1:T(2,128)(2,1)} fusion(bf16[1,1,2,8,2,32,2,512]{7,6,5,4,3,2,1,0:T(2,128)(2,1)S(1)} %stack.244, bf16[1,1,2,8,2,32,2,512]{7,6,5,4,3,2,1,0:T(2,128)(2,1)} %stack.243), kind=kLoop, calls=%fused_computation.50 | loop fusion | flops 2097152 | bytes 8388608 | tf_op jit(solution)/shard_map/transpose | solution.py:72
  95.4 8.0 %reshape_reshape.3 = bf16[512,4096]{1,0:T(8,128)(2,1)} reshape(bf16[2,1,8,32,2,2,2,512]{7,6,5,4,3,2,0,1:T(2,128)(2,1)} %copy_bitcast_fusion) | data formatting | bytes 8388608 | tf_op jit(solution)/shard_map/reshape;reshape | solution.py:89
  103.4 3.4 fusion.72
  107.0 1.3 collective-permute-start.8
  108.3 4.6 %collective-permute-start.7 = (bf16[2,1,8,32,256]{4,3,2,0,1:T(8,128)(2,1)S(1)}, bf16[2,1,8,32,256]{4,3,2,0,1:T(8,128)(2,1)S(1)}, u32[]{:S(2)}, u32[]{:S(2)}) collective-permute-start(bf16[2,1,8,32,256]{4,3,2,0,1:T(8,128)(2,1)S(1)} %pad_maximum_fusion.20), channel_id=1, source_target_pairs={{0,1},{1,2},{2,3},{3,4},{4,5},{5,6},{6,7},{8,9},{9,10},{10,11},{11... | collective-permute-start | bytes 786440 | tf_op jit(solution)/shard_map/ppermute | solution.py:12
  112.9 4.4 %collective-permute-done.8 = bf16[2,1,8,32,256]{4,3,2,0,1:T(8,128)(2,1)S(1)} collective-permute-done((bf16[2,1,8,32,256]{4,3,2,0,1:T(8,128)(2,1)S(1)}, bf16[2,1,8,32,256]{4,3,2,0,1:T(8,128)(2,1)S(1)}, u32[]{:S(2)}, u32[]{:S(2)}) %collective-permute-start.8) | collective-permute-done | bytes 262176 | tf_op jit(solution)/shard_map/ppermute | solution.py:15
  117.3 1.0 collective-permute-done.7
  118.3 1.0 pad_maximum_fusion.19
  119.4 4.0 %maximum_select_fusion.1 = bf16[27,256,256]{2,1,0:T(8,128)(2,1)S(1)} fusion(bf16[27,128,256]{2,1,0:T(8,128)(2,1)} %convert_element_type.49, bf16[27,128,256]{2,1,0:T(8,128)(2,1)} %collective-permute-done.9, pred[]{:T(512)S(6)} %eq.10), kind=kLoop, calls=%fused_computation.51 | loop fusion | flops 15925248 | bytes 7077889 | tf_op jit(solution)/shard_map/jit(_where)/select_n | solution.py:108
  123.4 1.3 collective-permute-start.10
  124.7 1.9 copy.61
  126.8 95.5 %collective-permute-done.10 = bf16[27,256,256]{2,1,0:T(8,128)(2,1)} collective-permute-done((bf16[27,256,256]{2,1,0:T(8,128)(2,1)S(1)}, bf16[27,256,256]{2,1,0:T(8,128)(2,1)}, u32[]{:S(2)}, u32[]{:S(2)}) %collective-permute-start.10) | collective-permute-done | bytes 3538976 | tf_op jit(solution)/shard_map/ppermute | solution.py:27
  222.3 5.2 %maximum_select_fusion = bf16[27,512,256]{2,1,0:T(8,128)(2,1)S(1)} fusion(bf16[27,256,256]{2,1,0:T(8,128)(2,1)S(1)} %maximum_select_fusion.1, bf16[27,256,256]{2,1,0:T(8,128)(2,1)} %collective-permute-done.10, pred[]{:T(512)S(6)} %eq.9), kind=kLoop, calls=%fused_computation | loop fusion | flops 31850496 | bytes 14155777 | tf_op jit(solution)/shard_map/jit(_where)/select_n | solution.py:108
  227.5 1.9 fusion.70
  229.4 2.3 constant_dynamic-slice_fusion
  232.1 4.2 %fusion.17 = (bf16[2,1,8,32,1,512]{5,3,2,0,4,1:T(8,128)(2,1)S(1)}, bf16[2,1,8,32,1,512]{5,3,2,0,4,1:T(8,128)(2,1)S(1)}, bf16[2,1,8,32,1,512]{5,3,2,0,4,1:T(8,128...) fusion(bf16[2,3,8,32,512]{4,3,2,0,1:T(8,128)(2,1)S(1)} %get-tup, ...), kind=kLoop, calls=%fused_computation.91 | loop fusion | bytes 11534336 | tf_op jit(solution)/shard_map/stack | solution.py:42
  236.9 1.4 copy.51
  238.8 1.4 copy.50
  243.7 1.4 copy.49
  245.6 1.4 copy.48
  247.5 1.8 copy.47
  249.9 1.4 copy.46
  251.8 1.4 copy.45
  253.7 1.4 copy.44
  255.6 1.4 copy.43
  257.6 0.6 copy-done.2
  261.6 43.1 %collective-permute-done.11 = bf16[2,3,8,32,512]{4,3,2,0,1:T(8,128)(2,1)S(1)} collective-permute-done((bf16[2,3,8,32,512]{4,3,2,0,1:T(8,128)(2,1)S(1)}, bf16[2,3,8,32,512]{4,3,2,0,1:T(8,128)(2,1)S(1)}, u32[]{:S(2)}, u32[]{:S(2)}) %collective-permute-start.11) | collective-permute-done | bytes 1572896 | tf_op jit(solution)/shard_map/ppermute | solution.py:27
  305.6 1.5 copy.60
  308.2 1.4 copy.59
  310.1 3.9 %fusion.41 = (bf16[2,1,8,32,1,512]{5,3,2,0,4,1:T(8,128)(2,1)S(1)}, bf16[2,1,8,32,1,512]{5,3,2,0,4,1:T(8,128)(2,1)S(1)}, bf16[2,1,8,32,1,512]{5,3,2,0,4,1:T(8,128...) fusion(bf16[2,3,8,32,512]{4,3,2,0,1:T(8,128)(2,1)S(1)} %collect, ...), kind=kLoop, calls=%fused_computation.115 | loop fusion | bytes 11534336 | tf_op jit(solution)/shard_map/stack | solution.py:42
  314.3 1.4 copy.58
  316.5 1.4 copy.57
  318.8 1.4 copy.56
  320.7 1.4 copy.55
  322.9 1.4 copy.54
  324.8 1.6 copy.53
  326.9 1.4 copy.52
  329.4 0.6 fusion.86
  330.6 0.6 fusion.84
  331.7 0.6 fusion.82
  332.9 0.7 fusion.16
  333.7 0.6 fusion.73
  334.3 9.8 %collective-permute-done.12 = bf16[512,256]{1,0:T(8,128)(2,1)S(1)} collective-permute-done((bf16[512,256]{1,0:T(8,128)(2,1)S(1)}, bf16[512,256]{1,0:T(8,128)(2,1)S(1)}, u32[]{:S(2)}, u32[]{:S(2)}) %collective-permute-start.12) | collective-permute-done | bytes 262176 | tf_op jit(solution)/shard_map/ppermute | solution.py:27
  344.0 0.7 fusion.15
  345.2 0.7 pad_maximum_fusion.21
  345.9 21.0 %all-gather.12.cloned.1.call-done = bf16[2,256,1024]{2,1,0:T(8,128)(2,1)} async-done(((bf16[2,256,256]{2,1,0:T(8,128)(2,1)}), bf16[2,256,1024]{2,1,0:T(8,128)(2,1)}) %all-gather.12.cloned.1.call-update) | async-done | bytes 1048592 | tf_op jit(solution)/shard_map/all_gather | solution.py:133
  366.9 3.2 fusion
  370.2 1.3 copy.62
  371.6 1.3 copy.63
  (108 shorter events, 23.2 us)
Async XLA Ops:
  7.2 73.5 %all-gather.8.cloned.1.call-start = ((), (), s32[]{:S(2)}) async-start(), calls=%async_computation.1 | async-start | bytes 2621440 | tf_op jit(solution)/shard_map/all_gather | solution.py:66
  7.9 75.6 %all-gather.6.cloned.1.call-start = ((), (), s32[]{:S(2)}) async-start(), calls=%async_computation | async-start | bytes 2621440 | tf_op jit(solution)/shard_map/all_gather | solution.py:65
  9.0 12.4 %collective-permute-start = (bf16[8,64,256]{2,1,0:T(8,128)(2,1)S(1)}, bf16[8,64,256]{2,1,0:T(8,128)(2,1)S(1)}, u32[]{:S(2)}, u32[]{:S(2)}) collective-permute-start(bf16[8,64,256]{2,1,0:T(8,128)(2,1)S(1)} %convert_element_type.46), channel_id=1, source_target_pairs={{0,1},{1,2},{2,3},{3,4},{4,5},{5,6},{6,7},{7,0},{8,9},{9,10},{10,1... | collective-permute-start | bytes 786440 | tf_op jit(solution)/shard_map/ppermute | solution.py:82
  21.4 10.2 %collective-permute-start.1 = (bf16[8,64,256]{2,1,0:T(8,128)(2,1)S(1)}, bf16[8,64,256]{2,1,0:T(8,128)(2,1)S(1)}, u32[]{:S(2)}, u32[]{:S(2)}) collective-permute-start(bf16[8,64,256]{2,1,0:T(8,128)(2,1)S(1)} %collective-permute-done), channel_id=1, source_target_pairs={{0,1},{1,2},{2,3},{3,4},{4,5},{5,6},{6,7},{7,0},{8,9},{9,10},{10,1... | collective-permute-start | bytes 786440 | tf_op jit(solution)/shard_map/ppermute | solution.py:82
  31.6 9.3 %collective-permute-start.2 = (bf16[8,64,256]{2,1,0:T(8,128)(2,1)S(1)}, bf16[8,64,256]{2,1,0:T(8,128)(2,1)S(1)}, u32[]{:S(2)}, u32[]{:S(2)}) collective-permute-start(bf16[8,64,256]{2,1,0:T(8,128)(2,1)S(1)} %collective-permute-done.1), channel_id=1, source_target_pairs={{0,1},{1,2},{2,3},{3,4},{4,5},{5,6},{6,7},{7,0},{8,9},{9,10},{10,1... | collective-permute-start | bytes 786440 | tf_op jit(solution)/shard_map/ppermute | solution.py:82
  40.9 9.1 %collective-permute-start.3 = (bf16[8,64,256]{2,1,0:T(8,128)(2,1)S(1)}, bf16[8,64,256]{2,1,0:T(8,128)(2,1)S(1)}, u32[]{:S(2)}, u32[]{:S(2)}) collective-permute-start(bf16[8,64,256]{2,1,0:T(8,128)(2,1)S(1)} %collective-permute-done.2), channel_id=1, source_target_pairs={{0,1},{1,2},{2,3},{3,4},{4,5},{5,6},{6,7},{7,0},{8,9},{9,10},{10,1... | collective-permute-start | bytes 786440 | tf_op jit(solution)/shard_map/ppermute | solution.py:82
  40.9 188.5 %all-gather.10.cloned.1.call-start = ((), (), s32[]{:S(2)}) async-start(), calls=%async_computation.2 | async-start | bytes 3932160 | tf_op jit(solution)/shard_map/all_gather | solution.py:100
  50.0 9.1 %collective-permute-start.4 = (bf16[8,64,256]{2,1,0:T(8,128)(2,1)S(1)}, bf16[8,64,256]{2,1,0:T(8,128)(2,1)S(1)}, u32[]{:S(2)}, u32[]{:S(2)}) collective-permute-start(bf16[8,64,256]{2,1,0:T(8,128)(2,1)S(1)} %collective-permute-done.3), channel_id=1, source_target_pairs={{0,1},{1,2},{2,3},{3,4},{4,5},{5,6},{6,7},{7,0},{8,9},{9,10},{10,1... | collective-permute-start | bytes 786440 | tf_op jit(solution)/shard_map/ppermute | solution.py:82
  59.0 9.7 %collective-permute-start.5 = (bf16[8,64,256]{2,1,0:T(8,128)(2,1)S(1)}, bf16[8,64,256]{2,1,0:T(8,128)(2,1)S(1)}, u32[]{:S(2)}, u32[]{:S(2)}) collective-permute-start(bf16[8,64,256]{2,1,0:T(8,128)(2,1)S(1)} %collective-permute-done.4), channel_id=1, source_target_pairs={{0,1},{1,2},{2,3},{3,4},{4,5},{5,6},{6,7},{7,0},{8,9},{9,10},{10,1... | collective-permute-start | bytes 786440 | tf_op jit(solution)/shard_map/ppermute | solution.py:82
  68.7 9.2 %collective-permute-start.6 = (bf16[8,64,256]{2,1,0:T(8,128)(2,1)S(1)}, bf16[8,64,256]{2,1,0:T(8,128)(2,1)S(1)}, u32[]{:S(2)}, u32[]{:S(2)}) collective-permute-start(bf16[8,64,256]{2,1,0:T(8,128)(2,1)S(1)} %collective-permute-done.5), channel_id=1, source_target_pairs={{0,1},{1,2},{2,3},{3,4},{4,5},{5,6},{6,7},{7,0},{8,9},{9,10},{10,1... | collective-permute-start | bytes 786440 | tf_op jit(solution)/shard_map/ppermute | solution.py:82
  72.2 47.1 %collective-permute-start.9 = (bf16[27,128,256]{2,1,0:T(8,128)(2,1)}, bf16[27,128,256]{2,1,0:T(8,128)(2,1)}, u32[]{:S(2)}, u32[]{:S(2)}) collective-permute-start(bf16[27,128,256]{2,1,0:T(8,128)(2,1)} %convert_element_type.49), channel_id=1, source_target_pairs={{0,1},{1,0},{2,3},{3,2},{4,5},{5,4},{6,7},{7,6},{8,9},{9,8},{10,11... | collective-permute-start | bytes 5308424 | tf_op jit(solution)/shard_map/ppermute | solution.py:27
  77.9 1.0 copy-start.6
  95.4 8.0 %copy-start.7 = (bf16[8,512,256]{2,1,0:T(8,128)(2,1)S(1)}, bf16[8,512,256]{2,1,0:T(8,128)(2,1)}, u32[]{:S(2)}) copy-start(bf16[8,512,256]{2,1,0:T(8,128)(2,1)} %constant_dynamic-slice_fusion.2) | copy-start | bytes 6291460
  106.9 11.3 %copy-start.8 = (bf16[256,256]{1,0:T(8,128)(2,1)}, bf16[256,256]{1,0:T(8,128)(2,1)S(1)}, u32[]{:S(2)}) copy-start(bf16[256,256]{1,0:T(8,128)(2,1)S(1)} %get-tuple-element.71) | copy-start | bytes 393220
  107.0 11.3 %copy-start.10 = (bf16[256,256]{1,0:T(8,128)(2,1)}, bf16[256,256]{1,0:T(8,128)(2,1)S(1)}, u32[]{:S(2)}) copy-start(bf16[256,256]{1,0:T(8,128)(2,1)S(1)} %get-tuple-element.72) | copy-start | bytes 393220
  107.0 10.3 %collective-permute-start.8 = (bf16[2,1,8,32,256]{4,3,2,0,1:T(8,128)(2,1)S(1)}, bf16[2,1,8,32,256]{4,3,2,0,1:T(8,128)(2,1)S(1)}, u32[]{:S(2)}, u32[]{:S(2)}) collective-permute-start(bf16[2,1,8,32,256]{4,3,2,0,1:T(8,128)(2,1)S(1)} %pad_maximum_fusion.20), channel_id=1, source_target_pairs={{1,0},{2,1},{3,2},{4,3},{5,4},{6,5},{7,6},{9,8},{10,9},{11,10},{12... | collective-permute-start | bytes 786440 | tf_op jit(solution)/shard_map/ppermute | solution.py:15
  108.3 10.0 %collective-permute-start.7 = (bf16[2,1,8,32,256]{4,3,2,0,1:T(8,128)(2,1)S(1)}, bf16[2,1,8,32,256]{4,3,2,0,1:T(8,128)(2,1)S(1)}, u32[]{:S(2)}, u32[]{:S(2)}) collective-permute-start(bf16[2,1,8,32,256]{4,3,2,0,1:T(8,128)(2,1)S(1)} %pad_maximum_fusion.20), channel_id=1, source_target_pairs={{0,1},{1,2},{2,3},{3,4},{4,5},{5,6},{6,7},{8,9},{9,10},{10,11},{11... | collective-permute-start | bytes 786440 | tf_op jit(solution)/shard_map/ppermute | solution.py:12
  119.3 226.6 %all-gather.14.cloned.1.call-start = ((), (), s32[]{:S(2)}) async-start(), calls=%async_computation.4 | async-start | bytes 2359296 | tf_op jit(solution)/shard_map/all_gather | solution.py:135
  123.4 98.9 %collective-permute-start.10 = (bf16[27,256,256]{2,1,0:T(8,128)(2,1)S(1)}, bf16[27,256,256]{2,1,0:T(8,128)(2,1)}, u32[]{:S(2)}, u32[]{:S(2)}) collective-permute-start(bf16[27,256,256]{2,1,0:T(8,128)(2,1)S(1)} %maximum_select_fusion.1), channel_id=1, source_target_pairs={{0,2},{2,0},{1,3},{3,1},{4,6},{6,4},{5,7},{7,5},{8,10},{10,8},{9,1... | collective-permute-start | bytes 10616840 | tf_op jit(solution)/shard_map/ppermute | solution.py:27
  126.7 240.2 %all-gather.12.cloned.1.call-start = ((), (), s32[]{:S(2)}) async-start(), calls=%async_computation.3 | async-start | bytes 1310720 | tf_op jit(solution)/shard_map/all_gather | solution.py:133
  232.1 4.2 %copy-start.5 = (bf16[2,3,8,32,1024]{4,3,2,0,1:T(8,128)(2,1)S(1)}, bf16[2,3,8,32,1024]{4,3,2,0,1:T(8,128)(2,1)}, u32[]{:S(2)}) copy-start(bf16[2,3,8,32,1024]{4,3,2,0,1:T(8,128)(2,1)} %all-gather.10.cloned.1.call-done) | copy-start | bytes 9437188
  240.1 1.1 copy-start.4
  240.7 1.2 copy-start.3
  240.7 64.0 %collective-permute-start.11 = (bf16[2,3,8,32,512]{4,3,2,0,1:T(8,128)(2,1)S(1)}, bf16[2,3,8,32,512]{4,3,2,0,1:T(8,128)(2,1)S(1)}, u32[]{:S(2)}, u32[]{:S(2)}) collective-permute-start(bf16[2,3,8,32,512]{4,3,2,0,1:T(8,128)(2,1)S(1)} %get-tuple-element.11), channel_id=1, source_target_pairs={{0,4},{4,0},{1,5},{5,1},{2,6},{6,2},{3,7},{7,3},{8,12},{12,8},{9,1... | collective-permute-start | bytes 4718600 | tf_op jit(solution)/shard_map/ppermute | solution.py:27
  257.0 1.1 copy-start.2
  257.5 1.2 copy-start.1
  258.7 1.1 copy-start
  333.6 10.4 %collective-permute-start.12 = (bf16[512,256]{1,0:T(8,128)(2,1)S(1)}, bf16[512,256]{1,0:T(8,128)(2,1)S(1)}, u32[]{:S(2)}, u32[]{:S(2)}) collective-permute-start(bf16[512,256]{1,0:T(8,128)(2,1)S(1)} %fusion.16), channel_id=1, source_target_pairs={{0,4},{4,0},{1,5},{5,1},{2,6},{6,2},{3,7},{7,3},{8,12},{12,8},{9,1... | collective-permute-start | bytes 786440 | tf_op jit(solution)/shard_map/ppermute | solution.py:27
  344.0 0.9 copy-start.9
  344.0 1.0 copy-start.11
Sparse Core Ops, SparseCore 0:
  9.5 25.5 all-gather.7
  41.0 23.8 all-gather.5
  119.4 27.8 all-gather.9
  149.8 65.6 all-gather.13
  346.0 20.8 all-gather.11
